TPU v7x, 32 devices: a whole 2x2x4 slice. The times are simulated.
32 devices in a mesh: groups: 2 (over y), dp: 4 (over z), mp: 4 (over x, core).
Axes of the slice: x: 2, y: 2, z: 4, core: 2. Of those that a mesh axis runs over, the one named last changes fastest.
Arguments:
- qkv_home: bfloat16 [8, 764, 3, 3072], P(('groups', 'dp'), None, None, 'mp'), parts along dimension 0, may hold values from -6 to 6
- resid_home: bfloat16 [8, 764, 6144], P(('groups', 'dp'), None, 'mp'), parts along dimension 0, may hold values from -6 to 6
- out_weight: bfloat16 [3072, 6144], P('dp', 'mp'), may hold values from -0.109375 to 0.109375
- label_weight: bfloat16 [6144, 12288], P('mp', 'dp'), may hold values from -0.21875 to 0.21875
- label_bias: float32 [12288], P('dp'), may hold values from -5 to 5
- query_gain: float32 [128], replicated, may hold values from 0.25 to 1.75
- key_gain: float32 [128], replicated, may hold values from 0.25 to 1.75
- patch_counts: int32 [8, 4], P('groups'), parts along dimension 0, may hold values from 1 to 191, as said below
- move_plan: int32 [8, 4], P('groups'), parts along dimension 0, may hold values from 0 to 3, as said below
- segment_ids: int32 [8, 764], P(('groups', 'dp')), parts along dimension 0, may hold values from 0 to 4, as said below
Outputs:
- mixed: bfloat16 [8, 384, 6144], P(('groups', 'dp'), None, 'mp'), parts along dimension 0
- labels: float32 [8, 4, 12288], P(('groups', 'dp'), 'mp'), parts along dimension 0
There are 2 independent parts, one for each index of `groups`. A program takes and returns all parts, laid end to end along the dimension named above; an argument that names none is the same for every part. Nothing has to cross between parts.
Inputs may be any that keep to these rules, and one draw needn't show every extreme that they name: `patch_counts`: home row r holds its 4 images packed in the order j; every destination row receives exactly one image from every home row, 384 patches in all; every draw holds an image of 191 patches. Every row of move_plan is a permutation, and every destination row appears once in every column, so each destination receives one image from each home row. `segment_ids`: image j of home row r has id j on its patch_counts[r, j] slots, which follow those of image j - 1; slots after the last image have id 4.
All inputs are finite; a program needn't handle non-finite values.
Results may differ from a plain program's by a relative error of at most 0.0065.
Values may be sent and summed in bfloat16 or wider, within the bound.
A program may use at most 64 MiB of HBM per device.

v0:
```python
import math

import jax
import jax.numpy as jnp
from jax import lax
from jax.sharding import PartitionSpec as P

TOK = 384


EPSILON = 1e-06


def head_norm(values, norm_gain):
    center = values - jnp.mean(values, axis=-1, keepdims=True)
    spread = jnp.mean(center * center, axis=-1, keepdims=True)
    return center * lax.rsqrt(spread + EPSILON) * norm_gain


def attend(qkv_rows, seg_rows, query_gain, key_gain):
    length = qkv_rows.shape[0]
    head_width = query_gain.shape[0]
    head_count = qkv_rows.shape[2] // head_width
    split_parts = qkv_rows.reshape(length, 3, head_count, head_width)
    queries = head_norm(split_parts[:, 0].astype(jnp.float32), query_gain).astype(jnp.bfloat16)
    key_rows = head_norm(split_parts[:, 1].astype(jnp.float32), key_gain).astype(jnp.bfloat16)
    scores = jnp.einsum(
        "qhd,khd->hqk", queries, key_rows, preferred_element_type=jnp.float32
    ) / math.sqrt(head_width)
    same_image = seg_rows[:, None] == seg_rows[None, :]
    raised = jnp.where(same_image[None], jnp.exp(scores), 0.0)
    weights = (raised / jnp.sum(raised, axis=-1, keepdims=True)).astype(jnp.bfloat16)
    head_out = jnp.einsum(
        "hqk,khd->qhd", weights, split_parts[:, 2], preferred_element_type=jnp.float32
    )
    return head_out.reshape(length, head_count * head_width).astype(jnp.bfloat16)


def project(heads_local, resid_rows, out_weight):
    gathered = lax.all_gather(heads_local, "mp", axis=1, tiled=True)
    running = resid_rows.astype(jnp.float32) + jnp.dot(
        gathered,
        lax.all_gather(out_weight, "dp", axis=0, tiled=True),
        preferred_element_type=jnp.float32,
    )
    return running.astype(jnp.bfloat16)


def pool(row_mixed, seg_rows, count_row):
    images = count_row.shape[0]
    member_ids = lax.broadcasted_iota(jnp.int32, (images, seg_rows.shape[0]), 0)
    member = (member_ids == seg_rows[None, :]).astype(jnp.bfloat16)
    image_sums = jnp.dot(member, row_mixed, preferred_element_type=jnp.float32)
    return (image_sums / count_row[:, None].astype(jnp.float32)).astype(jnp.bfloat16)


def label_terms(pooled, label_weight):
    return jnp.einsum(
        "abd,dc->abc",
        lax.all_gather(pooled[None], "dp", axis=0, tiled=True),
        label_weight,
        preferred_element_type=jnp.float32,
    )


def pick(values, row_index, is_valid):
    taken = jnp.take(values, row_index, axis=0)
    taken = taken.reshape(is_valid.shape + values.shape[1:])
    keep_mask = is_valid.reshape(is_valid.shape + (1,) * (values.ndim - 1))
    return jnp.where(keep_mask, taken, jnp.zeros_like(taken))


def on_device(
    qkv_home,
    resid_home,
    out_weight,
    label_weight,
    label_bias,
    query_gain,
    key_gain,
    patch_counts,
    move_plan,
    segment_ids,
):
    row_count = lax.axis_size("dp")
    my_index = lax.axis_index("dp")
    home_slots = segment_ids.shape[1]
    pair_slots = home_slots // row_count
    image_ids = lax.broadcasted_iota(jnp.int32, (row_count, row_count, row_count), 2)
    image_ends = jnp.cumsum(patch_counts, axis=1)
    starts = image_ends - patch_counts
    matches = (move_plan[:, :, None] == image_ids).astype(jnp.int32)
    image_sizes = jnp.sum(patch_counts[:, :, None] * matches, axis=1)
    firsts = jnp.sum(starts[:, :, None] * matches, axis=1)
    send_sizes = lax.dynamic_index_in_dim(image_sizes, my_index, 0, keepdims=False)
    send_firsts = lax.dynamic_index_in_dim(firsts, my_index, 0, keepdims=False)
    within = lax.broadcasted_iota(jnp.int32, (row_count, pair_slots), 1)
    send_valid = within < send_sizes[:, None]
    send_index = jnp.minimum(send_firsts[:, None] + within, home_slots - 1).reshape(-1)
    arrive_sizes = lax.dynamic_index_in_dim(image_sizes, my_index, 1, keepdims=False)
    arrive_ends = jnp.cumsum(arrive_sizes)
    arrive_starts = arrive_ends - arrive_sizes
    slot_grid = lax.broadcasted_iota(jnp.int32, (TOK, row_count), 0)
    source = jnp.sum((slot_grid >= arrive_ends[None, :]).astype(jnp.int32), axis=1)
    chosen = (source[:, None] == lax.broadcasted_iota(jnp.int32, (TOK, row_count), 1)).astype(
        jnp.int32
    )
    arrive_index = (
        source * pair_slots + slot_grid[:, 0] - jnp.sum(chosen * arrive_starts[None, :], axis=1)
    )
    home_mixed = project(
        attend(qkv_home[0], segment_ids[0], query_gain, key_gain), resid_home[0], out_weight
    )
    count_row = lax.dynamic_index_in_dim(patch_counts, my_index, 0, keepdims=False)
    pooled = pool(home_mixed, segment_ids[0], count_row)
    partial_value = label_terms(pooled, label_weight)
    send_mixed = pick(home_mixed, send_index, send_valid)
    got_mixed = lax.all_to_all(send_mixed, "dp", split_axis=0, concat_axis=0, tiled=True)
    mixed = jnp.take(got_mixed.reshape(row_count * pair_slots, -1), arrive_index, axis=0)
    logit_sums = lax.psum_scatter(
        partial_value.astype(jnp.bfloat16), "mp", scatter_dimension=1, tiled=True
    ).astype(jnp.float32)
    class_probs = jax.nn.sigmoid(logit_sums + label_bias[None, None, :])
    labels = lax.all_to_all(
        class_probs.astype(jnp.bfloat16), "dp", split_axis=0, concat_axis=2, tiled=True
    ).astype(class_probs.dtype)
    return (mixed[None], labels)


def solution(mesh):
    return jax.shard_map(
        on_device,
        mesh=mesh,
        in_specs=(
            P(("groups", "dp"), None, None, "mp"),
            P(("groups", "dp"), None, "mp"),
            P("dp", "mp"),
            P("mp", "dp"),
            P("dp"),
            P(),
            P(),
            P("groups", None),
            P("groups", None),
            P(("groups", "dp"), None),
        ),
        out_specs=(P(("groups", "dp"), None, "mp"), P(("groups", "dp"), "mp", None)),
        check_vma=False,
    )
```

profile of v0, /device:TPU:0, one launch (start us, length us, event | category | flops | bytes accessed | tf_op | source)
XLA Modules:
  0.0 383.3 jit_solution(16641087347745729092)
XLA Ops:
  7.2 4.3 %copy.31 = bf16[1,764,3,768]{1,3,2,0:T(8,128)(2,1)S(1)} copy(bf16[1,764,3,768]{3,1,2,0:T(8,128)(2,1)} %param.10) | data formatting | bytes 7041024 | tf_op args[0]
  12.0 0.7 fusion.11
  12.7 0.6 add_rsqrt_fusion
  13.3 0.6 add_rsqrt_fusion.1
  13.9 0.4 broadcast_compare_fusion
  14.4 8.7 %fusion = (f32[6,764]{1,0:T(8,128)}, f32[6,764,764]{1,2,0:T(8,128)}) fusion(pred[764,764]{0,1:T(8,128)(4,1)S(1)} %broadcast_compare_fusion, f32[128]{0:T(128)S(1)} %copy-done.7, f32[764,6]{0,1:T(8,128)} %add_rsqrt_fusion, f32[764,6]{0,1:T(8,128)} %copy-done.1, bf16[764,3,6,128]{0,3,2,1:T(8,128)(2,1)S(1)} %bitcast.68, f32[128]{0:T(128)S(1)} %copy-done.8, ...), kind=kOutput, calls=%fused_computation.4 | convolution fusion | flops 912926592 | bytes 17050528 | tf_op jit(solution)/shard_map/qhd,khd->hqk/dot_general | solution.py:27
  23.0 8.3 %fusion.22 = bf16[6,764,128]{1,2,0:T(8,128)(2,1)} fusion(f32[6,764,764]{1,2,0:T(8,128)} %get-tuple-element.13, f32[6,764]{1,0:T(8,128)} %get-tuple-element.12, pred[764,764]{0,1:T(8,128)(4,1)} %copy-done, bf16[764,3,6,128]{0,3,2,1:T(8,128)(2,1)S(1)} %bitcast.69), kind=kOutput, calls=%fused_computation.31 | convolution fusion | flops 911152512 | bytes 16963888 | tf_op jit(solution)/shard_map/hqk,khd->qhd/dot_general | solution.py:33
  31.4 0.7 all-gather.7.cloned.1.call-update
  32.8 38.9 %all-gather.5.cloned.1.call-done = bf16[764,3072]{0,1:T(8,128)(2,1)} async-done(((bf16[764,768]{0,1:T(8,128)(2,1)}), bf16[764,3072]{0,1:T(8,128)(2,1)}) %all-gather.5.cloned.1.call-update) | async-done | bytes 4694032 | tf_op jit(solution)/shard_map/all_gather | solution.py:40
  71.7 168.4 %all-gather.7.cloned.1.call-done = bf16[3072,1536]{1,0:T(8,128)(2,1)} async-done(((bf16[768,1536]{1,0:T(8,128)(2,1)}), bf16[3072,1536]{1,0:T(8,128)(2,1)}) %all-gather.7.cloned.1.call-update) | async-done | bytes 9437200 | tf_op jit(solution)/shard_map/all_gather | solution.py:43
  240.1 12.0 %fusion.4 = bf16[764,1536]{1,0:T(8,128)(2,1)S(1)} fusion(bf16[764,3072]{0,1:T(8,128)(2,1)} %all-gather.5.cloned.1.call-done, bf16[3072,1536]{1,0:T(8,128)(2,1)} %all-gather.7.cloned.1.call-done, bf16[1,764,1536]{2,1,0:T(8,128)(2,1)} %param.11), kind=kOutput, calls=%fused_computation.9 | convolution fusion | flops 7213529088 | bytes 18825216 | tf_op jit(solution)/shard_map/dot_general | solution.py:41
  252.0 0.4 fusion.21
  252.4 13.3 %all-gather.1 = bf16[4,4,1536]{2,1,0:T(4,128)(2,1)S(1)} all-gather(bf16[1,4,1536]{2,1,0:T(4,128)(2,1)S(1)} %fusion.21), channel_id=2, replica_groups=mesh['groups'=2,'dp'=4,'mp'=4] {'dp'}, dimensions={0}, use_global_device_ids=true | all-gather | bytes 61440 | tf_op jit(solution)/shard_map/all_gather | solution.py:60
  265.8 5.1 %fusion.5 = bf16[4,4,3072]{2,1,0:T(4,128)(2,1)S(1)} fusion(bf16[4,4,1536]{2,1,0:T(4,128)(2,1)S(1)} %all-gather.1, bf16[1536,3072]{1,0:T(8,128)(2,1)} %param.13), kind=kOutput, calls=%fused_computation.10 | convolution fusion | flops 151044096 | bytes 9584640 | tf_op jit(solution)/shard_map/abd,dc->abc/dot_general | solution.py:58
  270.9 0.7 copy.35
  271.6 0.6 dynamic-slice
  272.2 3.8 gather_fusion
  276.0 2.3 gather.13
  278.3 23.2 %all-reduce.3.cloned.1.call-done = bf16[4,4,3072]{2,0,1:T(4,128)(2,1)} async-done(((bf16[4,4,3072]{2,0,1:T(4,128)(2,1)}), bf16[4,4,3072]{2,0,1:T(4,128)(2,1)}) %all-reduce.3.cloned.1.call-update) | async-done | bytes 98320
  301.5 1.4 fusion.34
  302.9 0.5 broadcast.206
  303.4 0.7 reduce.11
  304.1 0.6 reshape.285
  304.7 4.6 %all-to-all-start.1 = ((bf16[4,2,1536]{2,1,0:T(2,128)(2,1)}), bf16[4,2,1536]{2,1,0:T(2,128)(2,1)S(1)}, u32[]{:S(2)}, u32[]{:S(2)}) async-start(bf16[4,2,1536]{2,1,0:T(2,128)(2,1)} %reshape.285), calls=%async_computation.1 | async-start | bytes 49152 | tf_op jit(solution)/shard_map/all_to_all | solution.py:124
  309.3 1.7 select_select_fusion
  311.1 3.9 %all-to-all-done.1 = bf16[4,2,1536]{2,1,0:T(2,128)(2,1)S(1)} async-done(((bf16[4,2,1536]{2,1,0:T(2,128)(2,1)}), bf16[4,2,1536]{2,1,0:T(2,128)(2,1)S(1)}, u32[]{:S(2)}, u32[]{:S(2)}) %all-to-all-start.1) | async-done | bytes 24608 | tf_op jit(solution)/shard_map/all_to_all | solution.py:124
  315.0 4.5 %all-to-all-start = ((bf16[4,191,1536]{2,1,0:T(8,128)(2,1)}), bf16[4,191,1536]{2,1,0:T(8,128)(2,1)}, u32[]{:S(2)}, u32[]{:S(2)}) async-start(bf16[4,191,1536]{2,1,0:T(8,128)(2,1)} %select_select_fusion), calls=%async_computation | async-start | bytes 4718592 | tf_op jit(solution)/shard_map/all_to_all | solution.py:118
  320.1 0.7 convert.3
  320.7 50.3 %all-to-all-done = bf16[4,191,1536]{2,1,0:T(8,128)(2,1)} async-done(((bf16[4,191,1536]{2,1,0:T(8,128)(2,1)}), bf16[4,191,1536]{2,1,0:T(8,128)(2,1)}, u32[]{:S(2)}, u32[]{:S(2)}) %all-to-all-start) | async-done | bytes 2347040 | tf_op jit(solution)/shard_map/all_to_all | solution.py:118
  371.1 2.3 reshape.254
  373.4 2.2 gather_fusion.1
  375.6 1.2 bitcast_select_fusion
  (50 shorter events, 1.9 us)
Async XLA Ops:
  7.2 64.5 %all-gather.5.cloned.1.call-start = ((), (), s32[]{:S(2)}) async-start(), calls=%async_computation.2 | async-start | bytes 5898240 | tf_op jit(solution)/shard_map/all_gather | solution.py:40
  11.5 2.4 copy-start.5
  11.5 2.8 copy-start.7
  11.5 2.8 copy-start.8
  11.9 1.4 copy-start.1
  12.0 1.3 copy-start.2
  14.4 8.7 %copy-start = (pred[764,764]{0,1:T(8,128)(4,1)}, pred[764,764]{0,1:T(8,128)(4,1)S(1)}, u32[]{:S(2)}) copy-start(pred[764,764]{0,1:T(8,128)(4,1)S(1)} %broadcast_compare_fusion) | copy-start | bytes 1751092
  31.3 0.8 copy-start.3
  31.3 1.0 copy-start.6
  31.3 208.7 %all-gather.7.cloned.1.call-start = ((), (), s32[]{:S(2)}) async-start(), calls=%async_computation.3 | async-start | bytes 11796480 | tf_op jit(solution)/shard_map/all_gather | solution.py:43
  32.1 269.4 %all-reduce.3.cloned.1.call-start = ((), (), s32[]{:S(2)}) async-start(), calls=%async_computation.4 | async-start | bytes 196608
  265.8 5.8 %copy-start.9 = (u32[32]{0:T(128)S(1)}, u32[32]{0:T(128)}, u32[]{:S(2)}) copy-start(u32[32]{0:T(128)} %constant.81) | copy-start | bytes 388
  276.0 25.5 %copy-start.4 = (f32[3072]{0:T(1024)S(1)}, f32[3072]{0:T(1024)}, u32[]{:S(2)}) copy-start(f32[3072]{0:T(1024)} %param.14) | copy-start | bytes 36868
  304.7 10.2 %all-to-all-start.1 = ((bf16[4,2,1536]{2,1,0:T(2,128)(2,1)}), bf16[4,2,1536]{2,1,0:T(2,128)(2,1)S(1)}, u32[]{:S(2)}, u32[]{:S(2)}) async-start(bf16[4,2,1536]{2,1,0:T(2,128)(2,1)} %reshape.285), calls=%async_computation.1 | async-start | bytes 49152 | tf_op jit(solution)/shard_map/all_to_all | solution.py:124
  315.0 56.1 %all-to-all-start = ((bf16[4,191,1536]{2,1,0:T(8,128)(2,1)}), bf16[4,191,1536]{2,1,0:T(8,128)(2,1)}, u32[]{:S(2)}, u32[]{:S(2)}) async-start(bf16[4,191,1536]{2,1,0:T(8,128)(2,1)} %select_select_fusion), calls=%async_computation | async-start | bytes 4718592 | tf_op jit(solution)/shard_map/all_to_all | solution.py:118
Sparse Core Ops, SparseCore 0:
  31.4 40.2 all-gather.4
  73.3 166.7 all-gather.6
  271.7 29.7 all-reduce.2
where the time goes:
time: 384 us; the launch traced here: 383 us
  waiting for transfers between devices  285 us (74%)
  matrix products  34.4 us (9%)
  local copies, waits for them, and re-layouts  17.7 us (5%)
  between operations  14 us (4%)
  blocking collectives  13.3 us (3%)
  other arithmetic  9.38 us (2%)
  starting transfers between devices  9.2 us (2%)
    all_gather x1, waiting for transfers between devices, project(): lax.all_gather(out_weight, 'dp', axis=0, tiled=True)  168 us
    all_to_all x1, waiting for transfers between devices, on_device(): lax.all_to_all(send_mixed, 'dp', split_axis=0, concat_axis=0, tiled=True)  50.3 us
    all_gather x1, waiting for transfers between devices, project(): gathered = lax.all_gather(heads_local, 'mp', axis=1, tiled=True)  38.9 us
    unnamed x4, waiting for transfers between devices  23.9 us
    all_gather x1, blocking collectives, label_terms(): lax.all_gather(pooled[None], 'dp', axis=0, tiled=True)  13.3 us
    dot_general x1, matrix products, project(): jnp.dot(gathered, lax.all_gather(out_weight, 'dp', axis=0, tiled=True), p...  12 us
    dot_general x1, matrix products, attend(): jnp.einsum('qhd,khd->hqk', queries, key_rows, preferred_element_type=jnp....  8.66 us
    dot_general x1, matrix products, attend(): jnp.einsum('hqk,khd->qhd', weights, split_parts[:, 2], preferred_element_...  8.27 us
  transfers between devices with their start and end apart: 5, of which 5 were waited for; matrix products, arithmetic and copies ran while one was open for 3% of the time, Pallas kernels for 0%

commit v1 on v0

--- a/solution.py
+++ b/solution.py
@@ -1,8 +1,11 @@
+import functools
 import math
 
 import jax
 import jax.numpy as jnp
 from jax import lax
+from jax.experimental import pallas as pl
+from jax.experimental.pallas import tpu as pltpu
 from jax.sharding import PartitionSpec as P
 
 TOK = 384
@@ -70,6 +73,523 @@
     return jnp.where(keep_mask, taken, jnp.zeros_like(taken))
 
 
+MESH = pl.DeviceIdType.MESH
+LANES = 128
+TILE = 256
+
+
+def remote(src, dst, send_sem, recv_sem, where):
+    return pltpu.make_async_remote_copy(
+        src_ref=src,
+        dst_ref=dst,
+        send_sem=send_sem,
+        recv_sem=recv_sem,
+        device_id=where,
+        device_id_type=MESH,
+    )
+
+
+def normed(values, gain):
+    values = values.astype(jnp.float32)
+    center = values - jnp.mean(values, axis=-1, keepdims=True)
+    spread = jnp.mean(center * center, axis=-1, keepdims=True)
+    return (center * lax.rsqrt(spread + EPSILON) * gain).astype(jnp.bfloat16)
+
+
+def block_kernel(
+    sizes,
+    counts,
+    plan,
+    q_ref,
+    k_ref,
+    v_ref,
+    bias_ref,
+    qg_ref,
+    kg_ref,
+    resid_hbm,
+    w_hbm,
+    lw_hbm,
+    out_ref,
+    lab_ref,
+    nq,
+    nk,
+    hall,
+    wall,
+    acc,
+    mixed,
+    sbuf,
+    rbuf,
+    lwv,
+    resv,
+    pools,
+    lgs,
+    lrecv,
+    pbuf,
+    precv,
+    load_sem,
+    hs,
+    hr,
+    wzs,
+    wzr,
+    wys,
+    wyr,
+    ps,
+    pr,
+    ms,
+    mr,
+    ls,
+    lr,
+    bs,
+    br,
+):
+    rows, slots, pair = sizes
+    me = lax.axis_index("dp")
+    mp = lax.axis_index("mp")
+    group = lax.axis_index("groups")
+    other = 1 - group
+    core = lax.rem(mp, 2)
+    near = mp + 1 - 2 * core
+    side = lax.rem(mp + 2, 4)
+    far = lax.rem(near + 2, 4)
+    length, width = q_ref.shape
+    depth, cols = w_hbm.shape
+    half = cols // 2
+    pieces = width // TILE
+    images = rows
+
+    loads = [
+        pltpu.make_async_copy(w_hbm, wall.at[me], load_sem.at[0]),
+        pltpu.make_async_copy(resid_hbm, resv, load_sem.at[1]),
+        pltpu.make_async_copy(lw_hbm, lwv, load_sem.at[2]),
+    ]
+    for load in loads:
+        load.start()
+
+    barrier = pltpu.get_barrier_semaphore()
+    for k in range(1, 4):
+        pl.semaphore_signal(
+            barrier, inc=1, device_id={"mp": lax.rem(mp + k, 4)}, device_id_type=MESH
+        )
+    for k in range(1, rows):
+        pl.semaphore_signal(
+            barrier, inc=1, device_id={"dp": lax.rem(me + k, rows)}, device_id_type=MESH
+        )
+    pl.semaphore_signal(barrier, inc=1, device_id={"groups": other}, device_id_type=MESH)
+    pl.semaphore_wait(barrier, 3 + rows - 1 + 1)
+
+    def wpart(block, which, c):
+        return wall.at[block, pl.ds(c * TILE, TILE), pl.ds(pl.multiple_of(which * half, half), half)]
+
+    def own_part(c):
+        return w_hbm.at[pl.ds(c * TILE, TILE), pl.ds(pl.multiple_of(group * half, half), half)]
+
+    def zcopy(direction, step, c):
+        block = me - step if direction == 0 else me + step
+        peer = me + 1 if direction == 0 else me - 1
+        return remote(
+            own_part(c) if step == 0 else wpart(block, group, c),
+            wpart(block, group, c),
+            wzs.at[direction, step, c],
+            wzr.at[block, c],
+            {"dp": peer},
+        )
+
+    def can_send(direction, step):
+        if direction == 0:
+            return jnp.logical_and(me - step >= 0, me < rows - 1)
+        return jnp.logical_and(me + step < rows, me > 0)
+
+    def arrives(direction, step):
+        return me - step >= 0 if direction == 0 else me + step < rows
+
+    def ycopy(direction, step, c):
+        block = me - step if direction == 0 else me + step
+        part = wpart(block, group, c)
+        return remote(part, part, wys.at[direction, step, c], wyr.at[block, c], {"groups": other})
+
+    chunks = depth // TILE
+    for c in range(chunks):
+        for direction in range(2):
+
+            @pl.when(can_send(direction, 0))
+            def _(direction=direction, c=c):
+                zcopy(direction, 0, c).start()
+
+    def forward(step, c):
+        for direction in range(2):
+
+            @pl.when(arrives(direction, step))
+            def _(direction=direction):
+                block = me - step if direction == 0 else me + step
+                got = wpart(block, group, c)
+                remote(got, got, wzs.at[0, 0, 0], wzr.at[block, c], {"groups": other}).wait_recv()
+                ycopy(direction, step, c).start()
+                if step < rows - 1:
+
+                    @pl.when(can_send(direction, step))
+                    def _():
+                        zcopy(direction, step, c).start()
+
+    own_counts = [counts[me, j] for j in range(images)]
+    own_plan = [plan[me, j] for j in range(images)]
+    ends, starts, running = [], [], 0
+    for j in range(images):
+        starts.append(running)
+        running = running + own_counts[j]
+        ends.append(running)
+
+    def segment(index):
+        total = jnp.zeros(index.shape, jnp.int32)
+        for j in range(images):
+            total = total + (index >= ends[j]).astype(jnp.int32)
+        return total
+
+    key_seg = segment(lax.broadcasted_iota(jnp.int32, (1, length), 1))
+    heads = width // LANES
+    q_gain = qg_ref[...]
+    k_gain = kg_ref[...]
+
+    def norm_head(h, carry):
+        at = pl.ds(pl.multiple_of(h * LANES, LANES), LANES)
+        nq[:, at] = normed(q_ref[:, at], q_gain)
+        nk[:, at] = normed(k_ref[:, at], k_gain)
+        return carry
+
+    lax.fori_loop(0, heads, norm_head, 0)
+    scale = math.log2(math.e) / math.sqrt(LANES)
+    per_head = length // TILE
+
+    def hcopy(kind, p):
+        at = pl.ds(p * TILE, TILE)
+        block = side if kind == 2 else mp
+        part = hall.at[block, :, at]
+        peer = side if kind == 1 else near
+        return remote(part, part, hs.at[kind, p], hr.at[kind, p], {"mp": peer})
+
+    def hwait(kind, p):
+        block = (near, side, far)[kind]
+        part = hall.at[block, :, pl.ds(p * TILE, TILE)]
+        remote(part, part, hs.at[kind, p], hr.at[kind, p], {"mp": near}).wait_recv()
+
+    for p in range(pieces):
+
+        def attend_part(i, carry, p=p):
+            h = p * (TILE // LANES) + i // per_head
+            first = pl.multiple_of(lax.rem(i, per_head) * TILE, TILE)
+            at = pl.ds(pl.multiple_of(h * LANES, LANES), LANES)
+            scores = lax.dot_general(
+                nq[pl.ds(first, TILE), at],
+                nk[:, at],
+                (((1,), (1,)), ((), ())),
+                preferred_element_type=jnp.float32,
+            )
+            query_seg = segment(lax.broadcasted_iota(jnp.int32, (TILE, 1), 0) + first)
+            raised = jnp.where(query_seg == key_seg, jnp.exp2(scores * scale), 0.0)
+            total = jnp.sum(raised, axis=-1, keepdims=True)
+            weights = (raised * (1.0 / total)).astype(jnp.bfloat16)
+            result = jnp.dot(weights, v_ref[:, at], preferred_element_type=jnp.float32)
+            hall[mp, pl.ds(first, TILE), at] = result.astype(jnp.bfloat16)
+            return carry
+
+        lax.fori_loop(0, (TILE // LANES) * per_head, attend_part, 0)
+        hcopy(1, p).start()
+        hcopy(0, p).start()
+        if p < chunks:
+            forward(1, p)
+    for c in range(pieces, chunks):
+        forward(1, c)
+    for p in range(pieces):
+        hwait(1, p)
+        hcopy(2, p).start()
+    for p in range(pieces):
+        hwait(0, p)
+        hwait(2, p)
+
+    def add_block(block, fresh):
+        def tile(t, carry):
+            at = pl.ds(pl.multiple_of(t * TILE, TILE), TILE)
+            term = jnp.dot(hall[block], wall[block, :, at], preferred_element_type=jnp.float32)
+            if fresh:
+                acc[:, at] = term
+                acc[pl.ds(0, slots), at] += resv[:, at].astype(jnp.float32)
+            else:
+                acc[:, at] += term
+            return carry
+
+        lax.fori_loop(0, cols // TILE, tile, 0)
+
+    loads[0].wait()
+    loads[1].wait()
+    add_block(me, True)
+
+    def use(step):
+        for direction in range(2):
+
+            @pl.when(arrives(direction, step))
+            def _(direction=direction):
+                block = me - step if direction == 0 else me + step
+                for c in range(chunks):
+                    got = wpart(block, other, c)
+                    remote(
+                        got, got, wzs.at[0, 0, 0], wyr.at[block, c], {"groups": other}
+                    ).wait_recv()
+                add_block(block, False)
+
+    for step in range(2, rows):
+        for c in range(chunks):
+            forward(step, c)
+        use(step - 1)
+    use(rows - 1)
+
+    def finish(t, carry):
+        at = pl.ds(pl.multiple_of(t * TILE, TILE), TILE)
+        mixed[:, at] = acc[:, at].astype(jnp.bfloat16)
+        return carry
+
+    lax.fori_loop(0, cols // TILE, finish, 0)
+
+    pad_images = pools.shape[1]
+    image_at = lax.broadcasted_iota(jnp.int32, (pad_images, length), 0)
+    member = jnp.logical_and(image_at == key_seg, image_at < images).astype(jnp.bfloat16)
+    sums = jnp.dot(member, mixed[...], preferred_element_type=jnp.float32)
+    image_col = lax.broadcasted_iota(jnp.int32, (pad_images, 1), 0)
+    divisor = jnp.ones((pad_images, 1), jnp.float32)
+    for j in range(images):
+        divisor = jnp.where(image_col == j, own_counts[j].astype(jnp.float32), divisor)
+    pools[me] = (sums / divisor).astype(jnp.bfloat16)
+
+    def dp_peer(k):
+        return lax.rem(me + k, rows)
+
+    def dp_from(k):
+        return lax.rem(me + rows - k, rows)
+
+    def pcopy(k):
+        return remote(pools.at[me], pools.at[me], ps.at[k], pr.at[k], {"dp": dp_peer(k)})
+
+    for k in range(1, rows):
+        pcopy(k).start()
+
+    def mcopy(k):
+        return remote(sbuf.at[k], rbuf.at[me], ms.at[k], mr.at[k], {"dp": dp_peer(k)})
+
+    def mwait(k):
+        part = rbuf.at[dp_from(k)]
+        remote(part, part, ms.at[k], mr.at[k], {"dp": dp_peer(k)}).wait_recv()
+
+    patch = lax.broadcasted_iota(jnp.int32, (pair, length), 0)
+    slot = lax.broadcasted_iota(jnp.int32, (pair, length), 1)
+    for k in (2, 1, 3, 0) if rows == 4 else tuple(range(1, rows)) + (0,):
+        dest = dp_peer(k)
+        first, count = 0, 0
+        for j in range(images):
+            hit = (own_plan[j] == dest).astype(jnp.int32)
+            first = first + hit * starts[j]
+            count = count + hit * own_counts[j]
+        pick_rows = jnp.logical_and(slot == patch + first, patch < count).astype(jnp.bfloat16)
+
+        def choose(t, carry, k=k, pick_rows=pick_rows):
+            at = pl.ds(pl.multiple_of(t * TILE, TILE), TILE)
+            part = jnp.dot(pick_rows, mixed[:, at], preferred_element_type=jnp.float32)
+            sbuf[k, :, at] = part.astype(jnp.bfloat16)
+            return carry
+
+        lax.fori_loop(0, cols // TILE, choose, 0)
+        if k:
+            mcopy(k).start()
+
+    for k in range(1, rows):
+        part = pools.at[dp_from(k)]
+        remote(part, part, ps.at[k], pr.at[k], {"dp": dp_peer(k)}).wait_recv()
+    loads[2].wait()
+    group_rows = lgs.shape[1]
+    order_row = lax.broadcasted_iota(jnp.int32, (images * group_rows, rows * pad_images), 0)
+    order_col = lax.broadcasted_iota(jnp.int32, (images * group_rows, rows * pad_images), 1)
+    wanted = lax.rem(order_row, group_rows) * pad_images + order_row // group_rows
+    order = (order_col == wanted).astype(jnp.bfloat16)
+    pooled_all = pools[...].reshape(rows * pad_images, cols)
+    by_image = jnp.dot(order, pooled_all, preferred_element_type=jnp.float32).astype(jnp.bfloat16)
+    classes = lwv.shape[1]
+
+    def label_tile(t, carry):
+        at = pl.ds(pl.multiple_of(t * TILE, TILE), TILE)
+        part = jnp.dot(by_image, lwv[:, at], preferred_element_type=jnp.float32)
+        for j in range(images):
+            lgs[j, :, at] = part[j * group_rows : (j + 1) * group_rows]
+        return carry
+
+    lax.fori_loop(0, classes // TILE, label_tile, 0)
+
+    def lcopy(k):
+        peer = lax.rem(mp + k, 4)
+        return remote(lgs.at[peer], lrecv.at[k], ls.at[k], lr.at[k], {"mp": peer})
+
+    for k in range(1, 4):
+        lcopy(k).start()
+    for k in range(1, 4):
+        lcopy(k).wait_recv()
+    total = lgs[mp]
+    for k in range(1, 4):
+        total = total + lrecv[k]
+    probs = jax.nn.sigmoid(total + bias_ref[...])
+    for r in range(rows):
+        for t in range(classes // LANES):
+            pbuf[r, pl.ds(t, 1), :] = probs[r : r + 1, t * LANES : (t + 1) * LANES]
+
+    def bcopy(k):
+        peer = dp_peer(k)
+        return remote(pbuf.at[peer], precv.at[me], bs.at[k], br.at[k], {"dp": peer})
+
+    for k in range(1, rows):
+        bcopy(k).start()
+
+    arrive, offset = [], 0
+    for r in range(rows):
+        count = 0
+        for j in range(images):
+            count = count + (plan[r, j] == me).astype(jnp.int32) * counts[r, j]
+        arrive.append((offset, count))
+        offset = offset + count
+    for k in range(1, rows):
+        mwait(k)
+    rbuf[me] = sbuf[0]
+    tokens = out_ref.shape[0]
+    token = lax.broadcasted_iota(jnp.int32, (tokens, pair), 0)
+    within = lax.broadcasted_iota(jnp.int32, (tokens, pair), 1)
+    places = [
+        jnp.logical_and(within == token - begin, within < count).astype(jnp.bfloat16)
+        for begin, count in arrive
+    ]
+
+    def place(t, carry):
+        at = pl.ds(pl.multiple_of(t * TILE, TILE), TILE)
+        part = jnp.dot(places[0], rbuf[0, :, at], preferred_element_type=jnp.float32)
+        for r in range(1, rows):
+            part = part + jnp.dot(places[r], rbuf[r, :, at], preferred_element_type=jnp.float32)
+        out_ref[:, at] = part.astype(jnp.bfloat16)
+        return carry
+
+    lax.fori_loop(0, cols // TILE, place, 0)
+    for k in range(1, rows):
+        part = precv.at[dp_from(k)]
+        remote(part, part, bs.at[k], br.at[k], {"dp": dp_peer(k)}).wait_recv()
+    precv[me] = pbuf[me]
+    lab_ref[...] = precv[...]
+
+    for p in range(pieces):
+        for kind in range(3):
+            hcopy(kind, p).wait_send()
+    for step in range(rows):
+        for direction in range(2):
+            for c in range(chunks):
+                if step < rows - 1:
+
+                    @pl.when(can_send(direction, step))
+                    def _(direction=direction, step=step, c=c):
+                        zcopy(direction, step, c).wait_send()
+
+                if step > 0:
+
+                    @pl.when(arrives(direction, step))
+                    def _(direction=direction, step=step, c=c):
+                        ycopy(direction, step, c).wait_send()
+
+    for k in range(1, rows):
+        pcopy(k).wait_send()
+        mcopy(k).wait_send()
+        bcopy(k).wait_send()
+    for k in range(1, 4):
+        lcopy(k).wait_send()
+
+
+def round_up(value, step):
+    return -(-value // step) * step
+
+
+def fused(
+    qkv_home,
+    resid_home,
+    out_weight,
+    label_weight,
+    label_bias,
+    query_gain,
+    key_gain,
+    patch_counts,
+    move_plan,
+):
+    rows = lax.axis_size("dp")
+    slots, width = qkv_home.shape[1], qkv_home.shape[3]
+    depth, cols = out_weight.shape
+    classes = label_weight.shape[1]
+    length = round_up(slots, TILE)
+    pair = round_up(slots // rows, 16)
+    padded = jnp.pad(qkv_home[0], ((0, length - slots), (0, 0), (0, 0)))
+    queries, keys, values = padded[:, 0], padded[:, 1], padded[:, 2]
+    chunks, pieces = depth // TILE, width // TILE
+    bf16, f32 = jnp.bfloat16, jnp.float32
+    vmem = pl.BlockSpec(memory_space=pltpu.VMEM)
+    smem = pl.BlockSpec(memory_space=pltpu.SMEM)
+    hbm = pl.BlockSpec(memory_space=pl.ANY)
+    dma = pltpu.SemaphoreType.DMA
+    mixed, labels = pl.pallas_call(
+        functools.partial(block_kernel, (rows, slots, pair)),
+        out_shape=(
+            jax.ShapeDtypeStruct((TOK, cols), bf16),
+            jax.ShapeDtypeStruct((rows, classes // LANES, LANES), f32),
+        ),
+        in_specs=[smem, smem, vmem, vmem, vmem, vmem, vmem, vmem, hbm, hbm, hbm],
+        out_specs=(vmem, vmem),
+        scratch_shapes=[
+            pltpu.VMEM((length, width), bf16),
+            pltpu.VMEM((length, width), bf16),
+            pltpu.VMEM((4, length, width), bf16),
+            pltpu.VMEM((rows, depth, cols), bf16),
+            pltpu.VMEM((length, cols), f32),
+            pltpu.VMEM((length, cols), bf16),
+            pltpu.VMEM((rows, pair, cols), bf16),
+            pltpu.VMEM((rows, pair, cols), bf16),
+            pltpu.VMEM(label_weight.shape, bf16),
+            pltpu.VMEM((slots, cols), bf16),
+            pltpu.VMEM((rows, 16, cols), bf16),
+            pltpu.VMEM((rows, 8, classes), f32),
+            pltpu.VMEM((4, 8, classes), f32),
+            pltpu.VMEM((rows, classes // LANES, LANES), f32),
+            pltpu.VMEM((rows, classes // LANES, LANES), f32),
+            dma((3,)),
+            dma((3, pieces)),
+            dma((3, pieces)),
+            dma((2, rows, chunks)),
+            dma((rows, chunks)),
+            dma((2, rows, chunks)),
+            dma((rows, chunks)),
+            dma((rows,)),
+            dma((rows,)),
+            dma((rows,)),
+            dma((rows,)),
+            dma((4,)),
+            dma((4,)),
+            dma((rows,)),
+            dma((rows,)),
+        ],
+        compiler_params=pltpu.CompilerParams(
+            collective_id=0, has_side_effects=True, vmem_limit_bytes=63 * 1024 * 1024
+        ),
+    )(
+        patch_counts,
+        move_plan,
+        queries,
+        keys,
+        values,
+        label_bias[None],
+        query_gain[None],
+        key_gain[None],
+        resid_home[0],
+        out_weight,
+        label_weight,
+    )
+    return (mixed[None], labels.reshape(1, 1, rows * classes))
+
+
 def on_device(
     qkv_home,
     resid_home,
@@ -83,6 +603,18 @@
     segment_ids,
 ):
     row_count = lax.axis_size("dp")
+    if row_count == lax.axis_size("mp") == 4 and lax.axis_size("groups") == 2:
+        return fused(
+            qkv_home,
+            resid_home,
+            out_weight,
+            label_weight,
+            label_bias,
+            query_gain,
+            key_gain,
+            patch_counts,
+            move_plan,
+        )
     my_index = lax.axis_index("dp")
     home_slots = segment_ids.shape[1]
     pair_slots = home_slots // row_count

time: 384 us -> 163 us (0.42)
  waiting for transfers between devices: 285 us -> 0 us
  Pallas kernels: 0 us -> 156 us
  matrix products: 34.4 us -> 0 us
  between operations: 14 us -> 0.65 us
  blocking collectives: 13.3 us -> 0 us
  local copies, waits for them, and re-layouts: 17.7 us -> 6.89 us
  other arithmetic: 9.38 us -> 0 us
  starting transfers between devices: 9.2 us -> 0 us
    all_gather x2 -> x0, waiting for transfers between devices: 207 us -> none  [the longest x1 168 us: project(): lax.all_gather(out_weight, 'dp', axis=0, tiled=True)]
    pallas_call x0 -> x1, Pallas kernels: none -> 156 us  [fused(): pl.pallas_call(functools.partial(block_kernel, (rows, slots, pair)), out_...]
    all_to_all x2 -> x0, waiting for transfers between devices: 54.2 us -> none  [the longest x1 50.3 us: on_device(): lax.all_to_all(send_mixed, 'dp', split_axis=0, concat_axis=0, tiled=True)]
    dot_general x5 -> x0, matrix products: 34.4 us -> none  [the longest x1 12 us: project(): jnp.dot(gathered, lax.all_gather(out_weight, 'dp', axis=0, tiled=True), p...]
    unnamed x4 -> x0, waiting for transfers between devices: 23.9 us -> none
    all_gather x1 -> x0, blocking collectives: 13.3 us -> none  [label_terms(): lax.all_gather(pooled[None], 'dp', axis=0, tiled=True)]
    all_to_all x2 -> x0, starting transfers between devices: 9.08 us -> none  [the longest x1 4.6 us: on_device(): lax.all_to_all(class_probs.astype(jnp.bfloat16), 'dp', split_axis=0, conc...]
    gather x3 -> x0, local copies, waits for them, and re-layouts: 8.32 us -> none  [the longest x2 6.09 us: pick(): taken = jnp.take(values, row_index, axis=0)]
  transfers between devices with their start and end apart: 5 -> 0, of which waited for: 5 -> 0; matrix products, arithmetic and copies ran while one was open for 3% -> 0% of each run, Pallas kernels for 0% -> 0%
where the time goes in v1:
time: 163 us
  Pallas kernels  156 us (96%)
  local copies, waits for them, and re-layouts  6.89 us (4%)
    pallas_call x1, Pallas kernels, fused(): pl.pallas_call(functools.partial(block_kernel, (rows, slots, pair)), out_...  156 us
    squeeze x1, local copies, waits for them, and re-layouts, fused(): queries, keys, values = (padded[:, 0], padded[:, 1], padded[:, 2])  3.89 us

profile of v1, /device:TPU:0, one launch (start us, length us, event | category | flops | bytes accessed | tf_op | source)
XLA Modules:
  0.0 163.2 jit_solution(9374305945179966677)
XLA Ops:
  0.6 3.9 %fusion.2 = (bf16[768,768]{1,0:T(8,128)(2,1)}, bf16[768,768]{1,0:T(8,128)(2,1)}, bf16[768,768]{1,0:T(8,128)(2,1)}) fusion(bf16[764,3,768]{2,0,1:T(8,128)(2,1)} %bitcast.13), kind=kLoop, calls=%fused_computation.5 | loop fusion | bytes 7059456 | tf_op jit(solution)/shard_map/squeeze | solution.py:527
  4.5 155.7 %shard_map.104 = (bf16[384,1536]{1,0:T(8,128)(2,1)}, f32[4,24,128]{2,1,0:T(8,128)}) custom-call(s32[4,4]{1,0:T(4,128)} %counts.1, s32[4,4]{1,0:T(4,128)} %plan.1, bf16[768,768]{1,0:T(8,128)(2,1)} %get-tuple-element.8.q_ref, bf16[768,768]{1,0:T(8,128)(2,1)} %get-tuple-element.7.k_ref, bf16[768,768]{1,0:T(8,128)(2,1)} %get-tuple-element.6.v_ref, ...), custom_call_target="tpu_custom_call" | custom-call | tf_op jit(solution)/shard_map/pallas_call | solution.py:534
  160.2 0.0 copy-start
  160.2 2.4 %copy.13 = bf16[1,384,1536]{2,1,0:T(8,128)(2,1)} copy(bf16[1,384,1536]{2,1,0:T(8,128)(2,1)} %bitcast.15) | data formatting | bytes 2359296
  162.6 0.0 copy-done
  162.6 0.6 copy.14
Async XLA Ops:
  160.2 2.4 %copy-start = (f32[4,24,128]{2,1,0:T(8,128)S(1)}, f32[4,24,128]{2,1,0:T(8,128)}, u32[]{:S(2)}) copy-start(f32[4,24,128]{2,1,0:T(8,128)} %get-tuple-element.5) | copy-start | bytes 147460

commit v2 on v1

--- a/solution.py
+++ b/solution.py
@@ -100,19 +100,19 @@
     sizes,
     counts,
     plan,
-    q_ref,
-    k_ref,
-    v_ref,
     bias_ref,
     qg_ref,
     kg_ref,
+    qkv_hbm,
     resid_hbm,
     w_hbm,
     lw_hbm,
     out_ref,
     lab_ref,
+    raw,
     nq,
     nk,
+    nv,
     hall,
     wall,
     acc,
@@ -142,7 +142,7 @@
     bs,
     br,
 ):
-    rows, slots, pair = sizes
+    rows, slots, pair, length, phases = sizes
     me = lax.axis_index("dp")
     mp = lax.axis_index("mp")
     group = lax.axis_index("groups")
@@ -151,13 +151,15 @@
     near = mp + 1 - 2 * core
     side = lax.rem(mp + 2, 4)
     far = lax.rem(near + 2, 4)
-    length, width = q_ref.shape
+    width = raw.shape[2]
     depth, cols = w_hbm.shape
-    half = cols // 2
+    span = cols // phases
+    half = span // 2
     pieces = width // TILE
     images = rows
 
     loads = [
+        pltpu.make_async_copy(qkv_hbm, raw, load_sem.at[3]),
         pltpu.make_async_copy(w_hbm, wall.at[me], load_sem.at[0]),
         pltpu.make_async_copy(resid_hbm, resv, load_sem.at[1]),
         pltpu.make_async_copy(lw_hbm, lwv, load_sem.at[2]),
@@ -177,21 +179,25 @@
     pl.semaphore_signal(barrier, inc=1, device_id={"groups": other}, device_id_type=MESH)
     pl.semaphore_wait(barrier, 3 + rows - 1 + 1)
 
-    def wpart(block, which, c):
-        return wall.at[block, pl.ds(c * TILE, TILE), pl.ds(pl.multiple_of(which * half, half), half)]
-
-    def own_part(c):
-        return w_hbm.at[pl.ds(c * TILE, TILE), pl.ds(pl.multiple_of(group * half, half), half)]
-
-    def zcopy(direction, step, c):
-        block = me - step if direction == 0 else me + step
-        peer = me + 1 if direction == 0 else me - 1
+    def share(phase, which):
+        return pl.ds(pl.multiple_of(phase * span + which * half, half), half)
+
+    def wpart(block, phase, which, c):
+        return wall.at[block, pl.ds(c * TILE, TILE), share(phase, which)]
+
+    def source(direction, step):
+        return me - step if direction == 0 else me + step
+
+    def zcopy(direction, phase, step, c):
+        block = source(direction, step)
+        part = wpart(block, phase, group, c)
+        own = w_hbm.at[pl.ds(c * TILE, TILE), share(phase, group)]
         return remote(
-            own_part(c) if step == 0 else wpart(block, group, c),
-            wpart(block, group, c),
-            wzs.at[direction, step, c],
-            wzr.at[block, c],
-            {"dp": peer},
+            own if step == 0 else part,
+            part,
+            wzs.at[direction, phase, step, c],
+            wzr.at[phase, block, c],
+            {"dp": me + 1 if direction == 0 else me - 1},
         )
 
     def can_send(direction, step):
@@ -202,33 +208,46 @@
     def arrives(direction, step):
         return me - step >= 0 if direction == 0 else me + step < rows
 
-    def ycopy(direction, step, c):
-        block = me - step if direction == 0 else me + step
-        part = wpart(block, group, c)
-        return remote(part, part, wys.at[direction, step, c], wyr.at[block, c], {"groups": other})
+    def ycopy(direction, phase, step, c):
+        block = source(direction, step)
+        part = wpart(block, phase, group, c)
+        return remote(
+            part,
+            part,
+            wys.at[direction, phase, step, c],
+            wyr.at[phase, block, c],
+            {"groups": other},
+        )
 
     chunks = depth // TILE
-    for c in range(chunks):
-        for direction in range(2):
-
-            @pl.when(can_send(direction, 0))
-            def _(direction=direction, c=c):
-                zcopy(direction, 0, c).start()
-
-    def forward(step, c):
+
+    def send_own(phase):
+        for c in range(chunks):
+            for direction in range(2):
+
+                @pl.when(can_send(direction, 0))
+                def _(direction=direction, c=c):
+                    zcopy(direction, phase, 0, c).start()
+
+    def forward(phase, step, c):
         for direction in range(2):
 
             @pl.when(arrives(direction, step))
             def _(direction=direction):
-                block = me - step if direction == 0 else me + step
-                got = wpart(block, group, c)
-                remote(got, got, wzs.at[0, 0, 0], wzr.at[block, c], {"groups": other}).wait_recv()
-                ycopy(direction, step, c).start()
+                block = source(direction, step)
+                got = wpart(block, phase, group, c)
+                remote(
+                    got, got, wzs.at[0, 0, 0, 0], wzr.at[phase, block, c], {"groups": other}
+                ).wait_recv()
                 if step < rows - 1:
 
                     @pl.when(can_send(direction, step))
                     def _():
-                        zcopy(direction, step, c).start()
+                        zcopy(direction, phase, step, c).start()
+
+                ycopy(direction, phase, step, c).start()
+
+    send_own(0)
 
     own_counts = [counts[me, j] for j in range(images)]
     own_plan = [plan[me, j] for j in range(images)]
@@ -251,10 +270,16 @@
 
     def norm_head(h, carry):
         at = pl.ds(pl.multiple_of(h * LANES, LANES), LANES)
-        nq[:, at] = normed(q_ref[:, at], q_gain)
-        nk[:, at] = normed(k_ref[:, at], k_gain)
+        nq[pl.ds(0, slots), at] = normed(raw[0, :, at], q_gain)
+        nk[pl.ds(0, slots), at] = normed(raw[1, :, at], k_gain)
+        nv[pl.ds(0, slots), at] = raw[2, :, at]
         return carry
 
+    if length > slots:
+        low = slots // 16 * 16
+        for ref in (nq, nk, nv):
+            ref[pl.ds(low, length - low), :] = jnp.zeros((length - low, width), jnp.bfloat16)
+    loads[0].wait()
     lax.fori_loop(0, heads, norm_head, 0)
     scale = math.log2(math.e) / math.sqrt(LANES)
     per_head = length // TILE
@@ -287,7 +312,7 @@
             raised = jnp.where(query_seg == key_seg, jnp.exp2(scores * scale), 0.0)
             total = jnp.sum(raised, axis=-1, keepdims=True)
             weights = (raised * (1.0 / total)).astype(jnp.bfloat16)
-            result = jnp.dot(weights, v_ref[:, at], preferred_element_type=jnp.float32)
+            result = jnp.dot(weights, nv[:, at], preferred_element_type=jnp.float32)
             hall[mp, pl.ds(first, TILE), at] = result.astype(jnp.bfloat16)
             return carry
 
@@ -295,19 +320,18 @@
         hcopy(1, p).start()
         hcopy(0, p).start()
         if p < chunks:
-            forward(1, p)
+            forward(0, 1, p)
     for c in range(pieces, chunks):
-        forward(1, c)
+        forward(0, 1, c)
+    if phases > 1:
+        send_own(1)
     for p in range(pieces):
         hwait(1, p)
         hcopy(2, p).start()
-    for p in range(pieces):
-        hwait(0, p)
-        hwait(2, p)
-
-    def add_block(block, fresh):
+
+    def add_block(block, phase, fresh):
         def tile(t, carry):
-            at = pl.ds(pl.multiple_of(t * TILE, TILE), TILE)
+            at = pl.ds(pl.multiple_of(phase * span + t * TILE, TILE), TILE)
             term = jnp.dot(hall[block], wall[block, :, at], preferred_element_type=jnp.float32)
             if fresh:
                 acc[:, at] = term
@@ -316,47 +340,31 @@
                 acc[:, at] += term
             return carry
 
-        lax.fori_loop(0, cols // TILE, tile, 0)
-
-    loads[0].wait()
-    loads[1].wait()
-    add_block(me, True)
-
-    def use(step):
+        lax.fori_loop(0, span // TILE, tile, 0)
+
+    def use(phase, step):
+        if step == 0:
+            add_block(me, phase, True)
+            return
         for direction in range(2):
 
             @pl.when(arrives(direction, step))
             def _(direction=direction):
-                block = me - step if direction == 0 else me + step
+                block = source(direction, step)
                 for c in range(chunks):
-                    got = wpart(block, other, c)
+                    got = wpart(block, phase, other, c)
                     remote(
-                        got, got, wzs.at[0, 0, 0], wyr.at[block, c], {"groups": other}
+                        got, got, wzs.at[0, 0, 0, 0], wyr.at[phase, block, c], {"groups": other}
                     ).wait_recv()
-                add_block(block, False)
-
-    for step in range(2, rows):
-        for c in range(chunks):
-            forward(step, c)
-        use(step - 1)
-    use(rows - 1)
-
-    def finish(t, carry):
-        at = pl.ds(pl.multiple_of(t * TILE, TILE), TILE)
-        mixed[:, at] = acc[:, at].astype(jnp.bfloat16)
-        return carry
-
-    lax.fori_loop(0, cols // TILE, finish, 0)
+                add_block(block, phase, False)
 
     pad_images = pools.shape[1]
     image_at = lax.broadcasted_iota(jnp.int32, (pad_images, length), 0)
     member = jnp.logical_and(image_at == key_seg, image_at < images).astype(jnp.bfloat16)
-    sums = jnp.dot(member, mixed[...], preferred_element_type=jnp.float32)
     image_col = lax.broadcasted_iota(jnp.int32, (pad_images, 1), 0)
     divisor = jnp.ones((pad_images, 1), jnp.float32)
     for j in range(images):
         divisor = jnp.where(image_col == j, own_counts[j].astype(jnp.float32), divisor)
-    pools[me] = (sums / divisor).astype(jnp.bfloat16)
 
     def dp_peer(k):
         return lax.rem(me + k, rows)
@@ -367,41 +375,100 @@
     def pcopy(k):
         return remote(pools.at[me], pools.at[me], ps.at[k], pr.at[k], {"dp": dp_peer(k)})
 
-    for k in range(1, rows):
-        pcopy(k).start()
-
-    def mcopy(k):
-        return remote(sbuf.at[k], rbuf.at[me], ms.at[k], mr.at[k], {"dp": dp_peer(k)})
-
-    def mwait(k):
-        part = rbuf.at[dp_from(k)]
-        remote(part, part, ms.at[k], mr.at[k], {"dp": dp_peer(k)}).wait_recv()
+    def columns(phase):
+        return pl.ds(phase * span, span)
+
+    def mcopy(phase, k):
+        at = columns(phase)
+        return remote(
+            sbuf.at[k, :, at],
+            rbuf.at[me, :, at],
+            ms.at[phase, k],
+            mr.at[phase, k],
+            {"dp": dp_peer(k)},
+        )
+
+    def mwait(phase, k):
+        part = rbuf.at[dp_from(k), :, columns(phase)]
+        remote(part, part, ms.at[phase, k], mr.at[phase, k], {"dp": dp_peer(k)}).wait_recv()
 
     patch = lax.broadcasted_iota(jnp.int32, (pair, length), 0)
     slot = lax.broadcasted_iota(jnp.int32, (pair, length), 1)
-    for k in (2, 1, 3, 0) if rows == 4 else tuple(range(1, rows)) + (0,):
-        dest = dp_peer(k)
-        first, count = 0, 0
-        for j in range(images):
-            hit = (own_plan[j] == dest).astype(jnp.int32)
-            first = first + hit * starts[j]
-            count = count + hit * own_counts[j]
-        pick_rows = jnp.logical_and(slot == patch + first, patch < count).astype(jnp.bfloat16)
-
-        def choose(t, carry, k=k, pick_rows=pick_rows):
-            at = pl.ds(pl.multiple_of(t * TILE, TILE), TILE)
-            part = jnp.dot(pick_rows, mixed[:, at], preferred_element_type=jnp.float32)
-            sbuf[k, :, at] = part.astype(jnp.bfloat16)
+    far_first = sorted(range(1, rows), key=lambda k: -min(k, rows - k))
+
+    def finish(phase):
+        def pool_tile(t, carry):
+            at = pl.ds(pl.multiple_of(phase * span + t * TILE, TILE), TILE)
+            values = acc[:, at].astype(jnp.bfloat16)
+            mixed[:, at] = values
+            sums = jnp.dot(member, values, preferred_element_type=jnp.float32)
+            pools[me, :, at] = (sums / divisor).astype(jnp.bfloat16)
             return carry
 
-        lax.fori_loop(0, cols // TILE, choose, 0)
-        if k:
-            mcopy(k).start()
+        lax.fori_loop(0, span // TILE, pool_tile, 0)
+        if phase == phases - 1:
+            for k in range(1, rows):
+                pcopy(k).start()
+        for k in far_first + [0]:
+            dest = dp_peer(k)
+            first, count = 0, 0
+            for j in range(images):
+                hit = (own_plan[j] == dest).astype(jnp.int32)
+                first = first + hit * starts[j]
+                count = count + hit * own_counts[j]
+            pick_rows = jnp.logical_and(slot == patch + first, patch < count).astype(jnp.bfloat16)
+
+            def choose(t, carry, k=k, pick_rows=pick_rows):
+                at = pl.ds(pl.multiple_of(phase * span + t * TILE, TILE), TILE)
+                part = jnp.dot(pick_rows, mixed[:, at], preferred_element_type=jnp.float32)
+                if k:
+                    sbuf[k, :, at] = part.astype(jnp.bfloat16)
+                else:
+                    rbuf[me, :, at] = part.astype(jnp.bfloat16)
+                return carry
+
+            lax.fori_loop(0, span // TILE, choose, 0)
+            if k:
+                mcopy(phase, k).start()
+
+    events = [(phase, step) for phase in range(phases) for step in range(1, rows)]
+    events.sort(key=lambda e: (2 * e[0] + e[1], -e[0]))
+    ready = False
+    waiting = [(0, 1)]
+    done = set()
+
+    def consume(phase, step):
+        nonlocal ready
+        if not ready:
+            for p in range(pieces):
+                hwait(0, p)
+                hwait(2, p)
+            loads[1].wait()
+            loads[2].wait()
+            ready = True
+        if (phase, 0) not in done:
+            done.add((phase, 0))
+            use(phase, 0)
+        use(phase, step)
+        done.add((phase, step))
+        if all((phase, i) in done for i in range(rows)):
+            finish(phase)
+
+    for phase, step in events[1:]:
+        if step == 2 and phase > 0 and phase + 1 < phases:
+            send_own(phase + 1)
+        for c in range(chunks):
+            forward(phase, step, c)
+        waiting.append((phase, step))
+        if len(waiting) > 2:
+            consume(*waiting.pop(0))
+    for phase, step in waiting:
+        consume(phase, step)
 
     for k in range(1, rows):
         part = pools.at[dp_from(k)]
         remote(part, part, ps.at[k], pr.at[k], {"dp": dp_peer(k)}).wait_recv()
-    loads[2].wait()
+    loads[3].wait()
     group_rows = lgs.shape[1]
     order_row = lax.broadcasted_iota(jnp.int32, (images * group_rows, rows * pad_images), 0)
     order_col = lax.broadcasted_iota(jnp.int32, (images * group_rows, rows * pad_images), 1)
@@ -450,9 +517,6 @@
             count = count + (plan[r, j] == me).astype(jnp.int32) * counts[r, j]
         arrive.append((offset, count))
         offset = offset + count
-    for k in range(1, rows):
-        mwait(k)
-    rbuf[me] = sbuf[0]
     tokens = out_ref.shape[0]
     token = lax.broadcasted_iota(jnp.int32, (tokens, pair), 0)
     within = lax.broadcasted_iota(jnp.int32, (tokens, pair), 1)
@@ -461,15 +525,18 @@
         for begin, count in arrive
     ]
 
-    def place(t, carry):
-        at = pl.ds(pl.multiple_of(t * TILE, TILE), TILE)
+    def place(t, carry, phase=0):
+        at = pl.ds(pl.multiple_of(phase * span + t * TILE, TILE), TILE)
         part = jnp.dot(places[0], rbuf[0, :, at], preferred_element_type=jnp.float32)
         for r in range(1, rows):
             part = part + jnp.dot(places[r], rbuf[r, :, at], preferred_element_type=jnp.float32)
         out_ref[:, at] = part.astype(jnp.bfloat16)
         return carry
 
-    lax.fori_loop(0, cols // TILE, place, 0)
+    for phase in range(phases):
+        for k in range(1, rows):
+            mwait(phase, k)
+        lax.fori_loop(0, span // TILE, functools.partial(place, phase=phase), 0)
     for k in range(1, rows):
         part = precv.at[dp_from(k)]
         remote(part, part, bs.at[k], br.at[k], {"dp": dp_peer(k)}).wait_recv()
@@ -479,24 +546,26 @@
     for p in range(pieces):
         for kind in range(3):
             hcopy(kind, p).wait_send()
-    for step in range(rows):
-        for direction in range(2):
-            for c in range(chunks):
-                if step < rows - 1:
-
-                    @pl.when(can_send(direction, step))
-                    def _(direction=direction, step=step, c=c):
-                        zcopy(direction, step, c).wait_send()
-
-                if step > 0:
-
-                    @pl.when(arrives(direction, step))
-                    def _(direction=direction, step=step, c=c):
-                        ycopy(direction, step, c).wait_send()
+    for phase in range(phases):
+        for k in range(1, rows):
+            mcopy(phase, k).wait_send()
+        for step in range(rows):
+            for direction in range(2):
+                for c in range(chunks):
+                    if step < rows - 1:
+
+                        @pl.when(can_send(direction, step))
+                        def _(phase=phase, direction=direction, step=step, c=c):
+                            zcopy(direction, phase, step, c).wait_send()
+
+                    if step > 0:
+
+                        @pl.when(arrives(direction, step))
+                        def _(phase=phase, direction=direction, step=step, c=c):
+                            ycopy(direction, phase, step, c).wait_send()
 
     for k in range(1, rows):
         pcopy(k).wait_send()
-        mcopy(k).wait_send()
         bcopy(k).wait_send()
     for k in range(1, 4):
         lcopy(k).wait_send()
@@ -523,8 +592,7 @@
     classes = label_weight.shape[1]
     length = round_up(slots, TILE)
     pair = round_up(slots // rows, 16)
-    padded = jnp.pad(qkv_home[0], ((0, length - slots), (0, 0), (0, 0)))
-    queries, keys, values = padded[:, 0], padded[:, 1], padded[:, 2]
+    phases = 2
     chunks, pieces = depth // TILE, width // TILE
     bf16, f32 = jnp.bfloat16, jnp.float32
     vmem = pl.BlockSpec(memory_space=pltpu.VMEM)
@@ -532,14 +600,16 @@
     hbm = pl.BlockSpec(memory_space=pl.ANY)
     dma = pltpu.SemaphoreType.DMA
     mixed, labels = pl.pallas_call(
-        functools.partial(block_kernel, (rows, slots, pair)),
+        functools.partial(block_kernel, (rows, slots, pair, length, phases)),
         out_shape=(
             jax.ShapeDtypeStruct((TOK, cols), bf16),
             jax.ShapeDtypeStruct((rows, classes // LANES, LANES), f32),
         ),
-        in_specs=[smem, smem, vmem, vmem, vmem, vmem, vmem, vmem, hbm, hbm, hbm],
+        in_specs=[smem, smem, vmem, vmem, vmem, hbm, hbm, hbm, hbm],
         out_specs=(vmem, vmem),
         scratch_shapes=[
+            pltpu.VMEM((3, slots, width), bf16),
+            pltpu.VMEM((length, width), bf16),
             pltpu.VMEM((length, width), bf16),
             pltpu.VMEM((length, width), bf16),
             pltpu.VMEM((4, length, width), bf16),
@@ -555,17 +625,17 @@
             pltpu.VMEM((4, 8, classes), f32),
             pltpu.VMEM((rows, classes // LANES, LANES), f32),
             pltpu.VMEM((rows, classes // LANES, LANES), f32),
-            dma((3,)),
+            dma((4,)),
             dma((3, pieces)),
             dma((3, pieces)),
-            dma((2, rows, chunks)),
-            dma((rows, chunks)),
-            dma((2, rows, chunks)),
-            dma((rows, chunks)),
+            dma((2, phases, rows, chunks)),
+            dma((phases, rows, chunks)),
+            dma((2, phases, rows, chunks)),
+            dma((phases, rows, chunks)),
             dma((rows,)),
             dma((rows,)),
-            dma((rows,)),
-            dma((rows,)),
+            dma((phases, rows)),
+            dma((phases, rows)),
             dma((4,)),
             dma((4,)),
             dma((rows,)),
@@ -577,12 +647,10 @@
     )(
         patch_counts,
         move_plan,
-        queries,
-        keys,
-        values,
         label_bias[None],
         query_gain[None],
         key_gain[None],
+        jnp.transpose(qkv_home[0], (1, 0, 2)),
         resid_home[0],
         out_weight,
         label_weight,

time: 163 us -> 146 us (0.90)
  Pallas kernels: 156 us -> 142 us
  local copies, waits for them, and re-layouts: 6.89 us -> 3 us
    pallas_call x1, Pallas kernels: 156 us -> 142 us  [fused(): pl.pallas_call(functools.partial(block_kernel, (rows, slots, pair, length...]
    squeeze x1 -> x0, local copies, waits for them, and re-layouts: 3.89 us -> none  [fused(): queries, keys, values = (padded[:, 0], padded[:, 1], padded[:, 2])]
where the time goes in v2:
time: 146 us
  Pallas kernels  142 us (97%)
  local copies, waits for them, and re-layouts  3 us (2%)
    pallas_call x1, Pallas kernels, fused(): pl.pallas_call(functools.partial(block_kernel, (rows, slots, pair, length...  142 us
    unnamed x4, local copies, waits for them, and re-layouts  3 us

profile of v2, /device:TPU:0, one launch (start us, length us, event | category | flops | bytes accessed | tf_op | source)
XLA Modules:
  0.0 145.8 jit_solution(5590396989456666314)
XLA Ops:
  0.6 142.1 %shard_map.104 = (bf16[384,1536]{1,0:T(8,128)(2,1)}, f32[4,24,128]{2,1,0:T(8,128)}) custom-call(s32[4,4]{1,0:T(4,128)} %counts.1, s32[4,4]{1,0:T(4,128)} %plan.1, f32[1,3072]{1,0:T(1,128)} %bitcast.13, f32[1,128]{1,0:T(1,128)} %bitcast.14, f32[1,128]{1,0:T(1,128)} %bitcast.15, bf16[3,764,768]{2,1,0:T(8,128)(2,1)} %bitcast.9, bf16[764,1536]{1,0:T(8,128)(2,1)} %bitcast.10, ...), custom_call_target="tpu_custom_call" | custom-call | tf_op jit(solution)/shard_map/pallas_call | solution.py:602
  142.8 0.0 copy-start
  142.8 2.4 %copy.13 = bf16[1,384,1536]{2,1,0:T(8,128)(2,1)} copy(bf16[1,384,1536]{2,1,0:T(8,128)(2,1)} %bitcast.11) | data formatting | bytes 2359296
  145.1 0.0 copy-done
  145.2 0.6 copy.14
Async XLA Ops:
  142.8 2.4 %copy-start = (f32[4,24,128]{2,1,0:T(8,128)S(1)}, f32[4,24,128]{2,1,0:T(8,128)}, u32[]{:S(2)}) copy-start(f32[4,24,128]{2,1,0:T(8,128)} %get-tuple-element.5) | copy-start | bytes 147460
